TPU v7x, 32 devices: a whole 2x2x4 slice. The times are simulated.
32 devices in a mesh: row: 4 (over y, x), col: 8 (over z, core).
Axes of the slice: x: 2, y: 2, z: 4, core: 2. Of those that a mesh axis runs over, the one named last changes fastest.
Arguments:
- trailing_slab: bfloat16 [24576, 8192], P('row', 'col'), may hold values from -6 to 6
- panel_cols: bfloat16 [24576, 512], P('row', 'col'), may hold values from -0.25 to 0.25
- head_slab: bfloat16 [512, 8192], P('row', 'col'), may hold values from -6 to 6
- coupling: bfloat16 [2, 256, 256], replicated, may hold values from -0.25 to 0.25
- lower_inverses: bfloat16 [2, 256, 256], replicated, may hold values from -1.5 to 1.5, as said below
- upper_inverses: bfloat16 [2, 256, 256], replicated, may hold values from -1.5 to 1.5, as said below
Outputs:
- trailing: bfloat16 [24576, 8192], P('row', 'col')
Inputs may be any that keep to these rules, and one draw needn't show every extreme that they name: `lower_inverses`: each of the two [256, 256] blocks is lower triangular with unit diagonal. `upper_inverses`: each of the two [256, 256] blocks is upper triangular with diagonal between 0.5 and 1.5.
All inputs are finite; a program needn't handle non-finite values.
Results may differ from a plain program's by a relative error of at most 0.0067.
Values may be sent and summed in bfloat16 or wider, within the bound.
No kernel may reach another device: no remote copies, remote signals or barrier semaphores. Data moves between devices by JAX's collectives and lax.ppermute only.
A program may use at most 128 MiB of HBM per device.

v0:
```python
import jax
import jax.numpy as jnp
from jax import lax
from jax.sharding import PartitionSpec as P


def product(left, right):
    return jnp.dot(left, right, preferred_element_type=jnp.float32)


def factor_panel(panel_block, upper_mid, upper_inverses):
    width = upper_mid.shape[0]
    lower_first = product(panel_block[:, :width], upper_inverses[0]).astype(jnp.bfloat16)
    panel_second = (
        panel_block[:, width:].astype(jnp.float32) - product(lower_first, upper_mid)
    ).astype(jnp.bfloat16)
    lower_second = product(panel_second, upper_inverses[1]).astype(jnp.bfloat16)
    return jnp.concatenate([lower_first, lower_second], axis=1)


def apply_update(slab_part, lower_block, upper_both):
    result = slab_part.astype(jnp.float32) - product(lower_block, upper_both)
    return result.astype(jnp.bfloat16)


def on_device(trailing_slab, panel_cols, head_slab, coupling, lower_inverses, upper_inverses):
    width = coupling.shape[1]
    head_full = lax.all_gather(head_slab, "row", axis=0, tiled=True)
    upper_mid = product(lower_inverses[0], coupling[0]).astype(jnp.bfloat16)
    upper_first = product(lower_inverses[0], head_full[:width]).astype(jnp.bfloat16)
    lower_head = product(coupling[1], upper_inverses[0]).astype(jnp.bfloat16)
    head_second = (head_full[width:].astype(jnp.float32) - product(lower_head, upper_first)).astype(
        jnp.bfloat16
    )
    upper_second = product(lower_inverses[1], head_second).astype(jnp.bfloat16)
    upper_both = jnp.concatenate([upper_first, upper_second], axis=0)
    panel_full = lax.all_gather(panel_cols, "col", axis=1, tiled=True)
    lower_block = factor_panel(panel_full, upper_mid, upper_inverses)
    return apply_update(trailing_slab, lower_block, upper_both)


def solution(mesh):
    in_specs = (P("row", "col"), P("row", "col"), P("row", "col"), P(), P(), P())
    out_specs = P("row", "col")
    return jax.shard_map(
        on_device, mesh=mesh, in_specs=in_specs, out_specs=out_specs, check_vma=False
    )
```

profile of v0, /device:TPU:0, one launch (start us, length us, event | category | flops | bytes accessed | tf_op | source)
XLA Modules:
  0.0 133.2 jit_solution(17150895435019928692)
XLA Ops:
  6.5 0.0 all-gather.5.cloned.1.call-start
  6.5 0.7 all-gather.5.cloned.1.call-update
  7.3 0.0 all-gather.3.cloned.1.call-start
  7.3 0.7 all-gather.3.cloned.1.call-update
  8.0 1.2 convolution_convert_fusion.4
  9.2 1.2 convolution_convert_fusion.5
  10.3 0.0 copy-start.1
  10.3 28.1 %all-gather.5.cloned.1.call-done = bf16[512,1024]{1,0:T(8,128)(2,1)} async-done(((bf16[128,1024]{1,0:T(8,128)(2,1)}), bf16[512,1024]{1,0:T(8,128)(2,1)}) %all-gather.5.cloned.1.call-update) | async-done | bytes 1048592 | tf_op jit(solution)/shard_map/all_gather | solution.py:28
  38.4 1.4 %convolution_convert_fusion.3 = bf16[256,1024]{1,0:T(8,128)(2,1)S(1)} fusion(bf16[512,1024]{1,0:T(8,128)(2,1)} %all-gather.5.cloned.1.call-done, bf16[2,256,256]{2,1,0:T(8,128)(2,1)} %param.10), kind=kOutput, calls=%fused_computation.11 | convolution fusion | flops 134479872 | bytes 1179648 | tf_op jit(solution)/shard_map/dot_general | solution.py:8
  39.9 0.0 copy-start
  39.9 2.6 %fusion.6 = bf16[256,1024]{1,0:T(8,128)(2,1)} fusion(bf16[256,256]{1,0:T(8,128)(2,1)S(1)} %convolution_convert_fusion.4, bf16[256,1024]{1,0:T(8,128)(2,1)S(1)} %convolution_convert_fusion.3, bf16[512,1024]{1,0:T(8,128)(2,1)} %all-gather.5.cloned.1.call-done, bf16[2,256,256]{2,1,0:T(8,128)(2,1)} %param.10), kind=kOutput, calls=%fused_computation.13 | convolution fusion | flops 269484032 | bytes 1835008 | tf_op jit(solution)/shard_map/dot_general | solution.py:8
  42.5 0.0 copy-done
  42.5 62.3 %all-gather.3.cloned.1.call-done = bf16[6144,512]{0,1:T(8,128)(2,1)} async-done(((bf16[6144,64]{0,1:T(8,128)(2,1)}), bf16[6144,512]{0,1:T(8,128)(2,1)}) %all-gather.3.cloned.1.call-update) | async-done | bytes 6291472 | tf_op jit(solution)/shard_map/all_gather | solution.py:37
  104.8 2.9 %convolution_convert_fusion.1 = bf16[6144,256]{0,1:T(8,128)(2,1)S(1)} fusion(bf16[6144,512]{0,1:T(8,128)(2,1)} %all-gather.3.cloned.1.call-done, bf16[2,256,256]{2,1,0:T(8,128)(2,1)} %param.11), kind=kOutput, calls=%fused_computation.4 | convolution fusion | flops 806879232 | bytes 6422528 | tf_op jit(solution)/shard_map/dot_general | solution.py:8
  107.7 0.0 copy-done.1
  107.7 5.5 %convolution_convert_fusion = bf16[6144,256]{0,1:T(8,128)(2,1)} fusion(bf16[6144,256]{0,1:T(8,128)(2,1)S(1)} %convolution_convert_fusion.1, bf16[256,256]{1,0:T(8,128)(2,1)S(1)} %convolution_convert_fusion.5, bf16[6144,512]{0,1:T(8,128)(2,1)} %all-gather.3.cloned.1.call-done, bf16[2,256,256]{2,1,0:T(8,128)(2,1)S(1)} %copy-done.1), kind=kOutput, calls=%fused_computation.3 | convolution fusion | flops 1616904192 | bytes 9699328 | tf_op jit(solution)/shard_map/dot_general | solution.py:8
  113.2 13.2 %subtract_convert_fusion = bf16[6144,1024]{1,0:T(8,128)(2,1)} fusion(bf16[6144,1024]{1,0:T(8,128)(2,1)} %param.6, bf16[6144,256]{0,1:T(8,128)(2,1)} %convolution_convert_fusion, bf16[6144,256]{0,1:T(8,128)(2,1)S(1)} %convolution_convert_fusion.1, bf16[256,1024]{1,0:T(8,128)(2,1)} %fusion.6, bf16[256,1024]{1,0:T(8,128)(2,1)} %copy-done), kind=kOutput, calls=%fused_computation | convolution fusion | flops 6476005376 | bytes 32505856 | tf_op jit(solution)/shard_map/dot_general | solution.py:8
Async XLA Ops:
  6.5 31.9 %all-gather.5.cloned.1.call-start = ((), (), s32[]{:S(2)}) async-start(), calls=%async_computation.1 | async-start | bytes 1310720 | tf_op jit(solution)/shard_map/all_gather | solution.py:28
  7.3 97.5 %all-gather.3.cloned.1.call-start = ((), (), s32[]{:S(2)}) async-start(), calls=%async_computation | async-start | bytes 7077888 | tf_op jit(solution)/shard_map/all_gather | solution.py:37
  10.3 97.4 %copy-start.1 = (bf16[2,256,256]{2,1,0:T(8,128)(2,1)S(1)}, bf16[2,256,256]{2,1,0:T(8,128)(2,1)}, u32[]{:S(2)}) copy-start(bf16[2,256,256]{2,1,0:T(8,128)(2,1)} %param.11) | copy-start | bytes 786436
  39.9 2.6 %copy-start = (bf16[256,1024]{1,0:T(8,128)(2,1)}, bf16[256,1024]{1,0:T(8,128)(2,1)S(1)}, u32[]{:S(2)}) copy-start(bf16[256,1024]{1,0:T(8,128)(2,1)S(1)} %convolution_convert_fusion.3) | copy-start | bytes 1572868
Sparse Core Ops, SparseCore 0:
  9.2 29.2 all-gather.4
  40.1 64.6 all-gather.2
where the time goes:
time: 133 us
  waiting for transfers between devices  91.8 us (69%)
  matrix products  27.9 us (21%)
  between operations  13.5 us (10%)
    all_gather x1, waiting for transfers between devices, on_device(): panel_full = lax.all_gather(panel_cols, 'col', axis=1, tiled=True)  62.3 us
    all_gather x1, waiting for transfers between devices, on_device(): head_full = lax.all_gather(head_slab, 'row', axis=0, tiled=True)  28.1 us
    dot_general x7, matrix products, product(): return jnp.dot(left, right, preferred_element_type=jnp.float32)  27.9 us
  transfers between devices with their start and end apart: 2, of which 2 were waited for; matrix products, arithmetic and copies ran while one was open for 5% of the time, Pallas kernels for 0%

commit v1 on v0

--- a/solution.py
+++ b/solution.py
@@ -25,7 +25,26 @@
 
 def on_device(trailing_slab, panel_cols, head_slab, coupling, lower_inverses, upper_inverses):
     width = coupling.shape[1]
-    head_full = lax.all_gather(head_slab, "row", axis=0, tiled=True)
+    size, place, rows = (lax.axis_size("row"), lax.axis_index("row"), head_slab.shape[0])
+    right_2 = [(i, (i + 1) % size) for i in range(size)]
+    left_2 = [(i, (i - 1) % size) for i in range(size)]
+    result_2 = jnp.zeros(
+        (*head_slab.shape[:0], size * rows, *head_slab.shape[0 + 1 :]), head_slab.dtype
+    )
+    result_2 = lax.dynamic_update_slice_in_dim(result_2, head_slab, place * rows, axis=0)
+    from_left = from_right = head_slab
+    half = size // 2
+    for step in range(1, half + 1):
+        from_left = lax.ppermute(from_left, "row", right_2)
+        result_2 = lax.dynamic_update_slice_in_dim(
+            result_2, from_left, (place - step) % size * rows, axis=0
+        )
+        if step < size - half:
+            from_right = lax.ppermute(from_right, "row", left_2)
+            result_2 = lax.dynamic_update_slice_in_dim(
+                result_2, from_right, (place + step) % size * rows, axis=0
+            )
+    head_full = result_2
     upper_mid = product(lower_inverses[0], coupling[0]).astype(jnp.bfloat16)
     upper_first = product(lower_inverses[0], head_full[:width]).astype(jnp.bfloat16)
     lower_head = product(coupling[1], upper_inverses[0]).astype(jnp.bfloat16)

time: 133 us -> 105 us (0.79)
  waiting for transfers between devices: 91.8 us -> 58.4 us
  starting transfers between devices: 0.04 us -> 5.11 us
    all_gather x1 -> x0, waiting for transfers between devices: 28.1 us -> none  [on_device(): head_full = lax.all_gather(head_slab, 'row', axis=0, tiled=True)]
    all_gather x1, waiting for transfers between devices: 62.3 us -> 43.4 us  [on_device(): panel_full = lax.all_gather(panel_cols, 'col', axis=1, tiled=True)]
    ppermute x0 -> x3, waiting for transfers between devices: none -> 14.2 us  [the longest x2 10.3 us: on_device(): from_left = lax.ppermute(from_left, 'row', right_2)]
    ppermute x0 -> x3, starting transfers between devices: none -> 5.1 us  [the longest x2 4.08 us: on_device(): from_left = lax.ppermute(from_left, 'row', right_2)]
  transfers between devices with their start and end apart: 2 -> 4, of which waited for: 2 -> 4; matrix products, arithmetic and copies ran while one was open for 5% -> 6% of each run, Pallas kernels for 0% -> 0%
where the time goes in v1:
time: 105 us
  waiting for transfers between devices  58.4 us (56%)
  matrix products  26.7 us (25%)
  between operations  13.5 us (13%)
  starting transfers between devices  5.11 us (5%)
  local copies, waits for them, and re-layouts  1.17 us (1%)
    all_gather x1, waiting for transfers between devices, on_device(): panel_full = lax.all_gather(panel_cols, 'col', axis=1, tiled=True)  43.4 us
    dot_general x7, matrix products, product(): return jnp.dot(left, right, preferred_element_type=jnp.float32)  26.7 us
    ppermute x2, waiting for transfers between devices, on_device(): from_left = lax.ppermute(from_left, 'row', right_2)  10.3 us
    ppermute x2, starting transfers between devices, on_device(): from_left = lax.ppermute(from_left, 'row', right_2)  4.08 us
    ppermute x1, waiting for transfers between devices, on_device(): from_right = lax.ppermute(from_right, 'row', left_2)  3.89 us
  transfers between devices with their start and end apart: 4, of which 4 were waited for; matrix products, arithmetic and copies ran while one was open for 6% of the time, Pallas kernels for 0%

profile of v1, /device:TPU:0, one launch (start us, length us, event | category | flops | bytes accessed | tf_op | source)
XLA Modules:
  0.0 104.9 jit_solution(3216653238825906955)
XLA Ops:
  6.5 0.0 copy-start.1
  6.5 0.0 copy-start.2
  6.5 0.0 all-gather.2.cloned.1.call-start
  6.5 0.7 all-gather.2.cloned.1.call-update
  7.3 3.0 %collective-permute-start = (bf16[128,1024]{1,0:T(8,128)(2,1)}, bf16[128,1024]{1,0:T(8,128)(2,1)S(1)}, u32[]{:S(2)}, u32[]{:S(2)}) collective-permute-start(bf16[128,1024]{1,0:T(8,128)(2,1)} %param.8), channel_id=1, source_target_pairs={{0,8},{8,16},{16,24},{24,0},{1,9},{9,17},{17,25},{25,1},{2,10},{10... | collective-permute-start | bytes 786440 | tf_op jit(solution)/shard_map/ppermute | solution.py:38
  10.3 1.0 collective-permute-start.1
  11.3 1.2 %convolution_convert_fusion.5 = bf16[256,256]{1,0:T(8,128)(2,1)S(1)} fusion(bf16[2,256,256]{2,1,0:T(8,128)(2,1)} %param.9, bf16[2,256,256]{2,1,0:T(8,128)(2,1)} %param.10), kind=kOutput, calls=%fused_computation.13 | convolution fusion | flops 33619968 | bytes 393216 | tf_op jit(solution)/shard_map/dot_general | solution.py:8
  12.5 6.1 %collective-permute-done = bf16[128,1024]{1,0:T(8,128)(2,1)S(1)} collective-permute-done((bf16[128,1024]{1,0:T(8,128)(2,1)}, bf16[128,1024]{1,0:T(8,128)(2,1)S(1)}, u32[]{:S(2)}, u32[]{:S(2)}) %collective-permute-start) | collective-permute-done | bytes 262176 | tf_op jit(solution)/shard_map/ppermute | solution.py:38
  18.6 1.1 %collective-permute-start.2 = (bf16[128,1024]{1,0:T(8,128)(2,1)S(1)}, bf16[128,1024]{1,0:T(8,128)(2,1)S(1)}, u32[]{:S(2)}, u32[]{:S(2)}) collective-permute-start(bf16[128,1024]{1,0:T(8,128)(2,1)S(1)} %collective-permute-done), channel_id=1, source_target_pairs={{0,8},{8,16},{16,24},{24,0},{1,9},{9,17},{17,25},{25,1},{2,10},{10... | collective-permute-start | bytes 786440 | tf_op jit(solution)/shard_map/ppermute | solution.py:38
  19.7 0.1 broadcast_in_dim.3
  19.8 1.0 constant_dynamic-update-slice_fusion.3
  20.9 3.9 %collective-permute-done.1 = bf16[128,1024]{1,0:T(8,128)(2,1)S(1)} collective-permute-done((bf16[128,1024]{1,0:T(8,128)(2,1)}, bf16[128,1024]{1,0:T(8,128)(2,1)S(1)}, u32[]{:S(2)}, u32[]{:S(2)}) %collective-permute-start.1) | collective-permute-done | bytes 262176 | tf_op jit(solution)/shard_map/ppermute | solution.py:43
  24.8 4.2 %collective-permute-done.2 = bf16[128,1024]{1,0:T(8,128)(2,1)S(1)} collective-permute-done((bf16[128,1024]{1,0:T(8,128)(2,1)S(1)}, bf16[128,1024]{1,0:T(8,128)(2,1)S(1)}, u32[]{:S(2)}, u32[]{:S(2)}) %collective-permute-start.2) | collective-permute-done | bytes 262176 | tf_op jit(solution)/shard_map/ppermute | solution.py:38
  29.0 1.2 %convolution_convert_fusion.3 = bf16[1024,256]{0,1:T(8,128)(2,1)S(1)} fusion(bf16[512,1024]{1,0:T(8,128)(2,1)S(1)} %constant_dynamic-update-slice_fusion, bf16[2,256,256]{2,1,0:T(8,128)(2,1)} %param.10), kind=kOutput, calls=%fused_computation.10 | convolution fusion | flops 134479872 | bytes 1179648 | tf_op jit(solution)/shard_map/dot_general | solution.py:8
  30.3 0.0 copy-start
  30.3 1.6 %fusion.6 = f32[256,1024]{1,0:T(8,128)S(1)} fusion(bf16[1024,256]{0,1:T(8,128)(2,1)S(1)} %convolution_convert_fusion.3, bf16[2,256,256]{2,1,0:T(8,128)(2,1)} %param.9, bf16[2,256,256]{2,1,0:T(8,128)(2,1)} %param.11), kind=kOutput, calls=%fused_computation.14 | convolution fusion | flops 167837696 | bytes 1835008 | tf_op jit(solution)/shard_map/dot_general | solution.py:8
  31.9 0.0 copy-done.1
  31.9 1.1 %fusion.5 = bf16[256,1024]{1,0:T(8,128)(2,1)} fusion(f32[256,1024]{1,0:T(8,128)S(1)} %fusion.6, bf16[512,1024]{1,0:T(8,128)(2,1)S(1)} %constant_dynamic-update-slice_fusion, bf16[2,256,256]{2,1,0:T(8,128)(2,1)S(1)} %copy-done.1), kind=kOutput, calls=%fused_computation.11 | convolution fusion | flops 135266304 | bytes 2228224 | tf_op jit(solution)/shard_map/dot_general | solution.py:8
  33.0 0.0 copy-done
  33.0 43.4 %all-gather.2.cloned.1.call-done = bf16[6144,512]{0,1:T(8,128)(2,1)} async-done(((bf16[6144,64]{0,1:T(8,128)(2,1)}), bf16[6144,512]{0,1:T(8,128)(2,1)}) %all-gather.2.cloned.1.call-update) | async-done | bytes 6291472 | tf_op jit(solution)/shard_map/all_gather | solution.py:56
  76.4 0.0 copy-done.2
  76.4 2.9 %convolution_convert_fusion.1 = bf16[6144,256]{0,1:T(8,128)(2,1)S(1)} fusion(bf16[6144,512]{0,1:T(8,128)(2,1)} %all-gather.2.cloned.1.call-done, bf16[2,256,256]{2,1,0:T(8,128)(2,1)S(1)} %copy-done.2), kind=kOutput, calls=%fused_computation.4 | convolution fusion | flops 806879232 | bytes 6422528 | tf_op jit(solution)/shard_map/dot_general | solution.py:8
  79.3 5.5 %convolution_convert_fusion = bf16[6144,256]{0,1:T(8,128)(2,1)} fusion(bf16[6144,256]{0,1:T(8,128)(2,1)S(1)} %convolution_convert_fusion.1, bf16[256,256]{1,0:T(8,128)(2,1)S(1)} %convolution_convert_fusion.5, bf16[6144,512]{0,1:T(8,128)(2,1)} %all-gather.2.cloned.1.call-done, bf16[2,256,256]{2,1,0:T(8,128)(2,1)S(1)} %copy-done.2), kind=kOutput, calls=%fused_computation.3 | convolution fusion | flops 1616904192 | bytes 9699328 | tf_op jit(solution)/shard_map/dot_general | solution.py:8
  84.8 13.2 %subtract_convert_fusion = bf16[6144,1024]{1,0:T(8,128)(2,1)} fusion(bf16[6144,1024]{1,0:T(8,128)(2,1)} %param.6, bf16[6144,256]{0,1:T(8,128)(2,1)} %convolution_convert_fusion, bf16[6144,256]{0,1:T(8,128)(2,1)S(1)} %convolution_convert_fusion.1, bf16[256,1024]{1,0:T(8,128)(2,1)} %fusion.5, bf16[256,1024]{1,0:T(8,128)(2,1)} %bitcast.30), kind=kOutput, calls=%fused_computation | convolution fusion | flops 6476005376 | bytes 32505856 | tf_op jit(solution)/shard_map/dot_general | solution.py:8
  (3 shorter events, 0.1 us)
Async XLA Ops:
  6.5 25.3 %copy-start.1 = (bf16[2,256,256]{2,1,0:T(8,128)(2,1)S(1)}, bf16[2,256,256]{2,1,0:T(8,128)(2,1)}, u32[]{:S(2)}) copy-start(bf16[2,256,256]{2,1,0:T(8,128)(2,1)} %param.10) | copy-start | bytes 786436
  6.5 69.9 %copy-start.2 = (bf16[2,256,256]{2,1,0:T(8,128)(2,1)S(1)}, bf16[2,256,256]{2,1,0:T(8,128)(2,1)}, u32[]{:S(2)}) copy-start(bf16[2,256,256]{2,1,0:T(8,128)(2,1)} %param.11) | copy-start | bytes 786436
  6.5 69.9 %all-gather.2.cloned.1.call-start = ((), (), s32[]{:S(2)}) async-start(), calls=%async_computation | async-start | bytes 7077888 | tf_op jit(solution)/shard_map/all_gather | solution.py:56
  7.3 11.3 %collective-permute-start = (bf16[128,1024]{1,0:T(8,128)(2,1)}, bf16[128,1024]{1,0:T(8,128)(2,1)S(1)}, u32[]{:S(2)}, u32[]{:S(2)}) collective-permute-start(bf16[128,1024]{1,0:T(8,128)(2,1)} %param.8), channel_id=1, source_target_pairs={{0,8},{8,16},{16,24},{24,0},{1,9},{9,17},{17,25},{25,1},{2,10},{10... | collective-permute-start | bytes 786440 | tf_op jit(solution)/shard_map/ppermute | solution.py:38
  10.3 14.5 %collective-permute-start.1 = (bf16[128,1024]{1,0:T(8,128)(2,1)}, bf16[128,1024]{1,0:T(8,128)(2,1)S(1)}, u32[]{:S(2)}, u32[]{:S(2)}) collective-permute-start(bf16[128,1024]{1,0:T(8,128)(2,1)} %param.8), channel_id=1, source_target_pairs={{0,24},{8,0},{16,8},{24,16},{1,25},{9,1},{17,9},{25,17},{2,26},{10... | collective-permute-start | bytes 786440 | tf_op jit(solution)/shard_map/ppermute | solution.py:43
  18.6 10.4 %collective-permute-start.2 = (bf16[128,1024]{1,0:T(8,128)(2,1)S(1)}, bf16[128,1024]{1,0:T(8,128)(2,1)S(1)}, u32[]{:S(2)}, u32[]{:S(2)}) collective-permute-start(bf16[128,1024]{1,0:T(8,128)(2,1)S(1)} %collective-permute-done), channel_id=1, source_target_pairs={{0,8},{8,16},{16,24},{24,0},{1,9},{9,17},{17,25},{25,1},{2,10},{10... | collective-permute-start | bytes 786440 | tf_op jit(solution)/shard_map/ppermute | solution.py:38
  30.3 2.7 %copy-start = (bf16[1024,256]{0,1:T(8,128)(2,1)}, bf16[1024,256]{0,1:T(8,128)(2,1)S(1)}, u32[]{:S(2)}) copy-start(bf16[1024,256]{0,1:T(8,128)(2,1)S(1)} %convolution_convert_fusion.3) | copy-start | bytes 1572868
Sparse Core Ops, SparseCore 0:
  9.0 67.4 all-gather.1
